TPU v7x, 32 devices: a whole 2x2x4 slice. The times are simulated.
32 devices in a mesh: dp: 8 (over z, x), mp: 4 (over y, core).
Axes of the slice: x: 2, y: 2, z: 4, core: 2. Of those that a mesh axis runs over, the one named last changes fastest.
Arguments:
- images: bfloat16 [64, 196, 768], P('dp'), may hold values from -6 to 6
- group_ids: int32 [64, 1], P('dp'), may hold values from 0 to 15, as said below
- query_gradient: float32 [3072, 768], P('mp', 'dp'), may hold values from -6 to 6
- first_gain: float32 [768], replicated, may hold values from 0.5 to 1.5
- first_bias: float32 [768], replicated, may hold values from -1.5 to 1.5
- token_expand: bfloat16 [196, 384], P(None, 'mp'), may hold values from -0.4375 to 0.4375
- expand_bias: float32 [384], P('mp'), may hold values from -1.5 to 1.5
- token_reduce: bfloat16 [384, 196], P('mp'), may hold values from -0.3125 to 0.3125
- reduce_bias: float32 [196], replicated, may hold values from -1.5 to 1.5
- second_gain: float32 [768], replicated, may hold values from 0.5 to 1.5
- second_bias: float32 [768], replicated, may hold values from -1.5 to 1.5
- channel_expand: bfloat16 [768, 3072], P(None, 'mp'), may hold values from -0.21875 to 0.21875
- channel_bias: float32 [3072], P('mp'), may hold values from -1.5 to 1.5
- channel_reduce: bfloat16 [3072, 768], P('mp'), may hold values from -0.109375 to 0.109375
- output_bias: float32 [768], replicated, may hold values from -1.5 to 1.5
- cotangent: bfloat16 [64, 196, 768], P('dp'), may hold values from -5.6 to 5.6
Outputs:
- block_output: bfloat16 [64, 196, 768], P('dp')
- input_grad: float32 [64, 196, 768], P('dp')
- first_gain_gradient: float32 [768], replicated
- first_bias_gradient: float32 [768], replicated
- token_expand_gradient: float32 [196, 384], P(None, 'mp')
- expand_bias_gradient: float32 [384], P('mp')
- token_reduce_gradient: float32 [384, 196], P('mp')
- reduce_bias_gradient: float32 [196], replicated
- second_gain_gradient: float32 [768], replicated
- second_bias_gradient: float32 [768], replicated
- channel_expand_gradient: float32 [768, 3072], P(None, 'mp')
- channel_bias_gradient: float32 [3072], P('mp')
- channel_reduce_gradient: float32 [3072, 768], P('mp', 'dp')
- output_bias_gradient: float32 [768], replicated
- group_norms: float32 [16], replicated
- influence: float32 [16], replicated
Inputs may be any that keep to these rules, and one draw needn't show every extreme that they name: `group_ids`: every one of the 16 groups marks at least one image.
All inputs are finite; a program needn't handle non-finite values.
Results may differ from a plain program's by a relative error of at most 0.02.
Values may be sent and summed in bfloat16 or wider, within the bound.
No kernel may reach another device: no remote copies, remote signals or barrier semaphores. Data moves between devices by JAX's collectives and lax.ppermute only.
A program may use at most 192 MiB of HBM per device.

v0:
```python
import jax
import jax.numpy as jnp
from jax import lax
from jax.sharding import PartitionSpec as P

GROUPS = 16
epsilon = 1e-06
highest = lax.Precision.HIGHEST


def norm_forward(inputs, norm_gain, norm_bias):
    center = inputs - jnp.mean(inputs, axis=-1, keepdims=True)
    inverse = lax.rsqrt(jnp.mean(center * center, axis=-1, keepdims=True) + epsilon)
    normal = center * inverse
    return (normal * norm_gain + norm_bias, normal, inverse)


def norm_backward(upstream, normal, inverse, norm_gain):
    scaled = upstream * norm_gain
    return inverse * (
        scaled
        - jnp.mean(scaled, axis=-1, keepdims=True)
        - normal * jnp.mean(scaled * normal, axis=-1, keepdims=True)
    )


def gelu_tanh(inputs):
    return jax.nn.gelu(inputs, approximate=True)


def gelu_back(inputs, upstream):
    unused, pullback = jax.vjp(gelu_tanh, inputs)
    return pullback(upstream)[0]


def per_device(
    images,
    group_ids,
    query_gradient,
    first_gain,
    first_bias,
    token_expand,
    expand_bias,
    token_reduce,
    reduce_bias,
    second_gain,
    second_bias,
    channel_expand,
    channel_bias,
    channel_reduce,
    output_bias,
    cotangent,
):
    batch = images.shape[0]
    patches = images.shape[1]
    width = images.shape[2]
    inputs = images.astype(jnp.float32)
    first_norm, first_normal, first_inverse = norm_forward(inputs, first_gain, first_bias)
    first_low = first_norm.astype(jnp.bfloat16)
    token_pre = (
        jnp.einsum("bsd,sh->bhd", first_low, token_expand, preferred_element_type=jnp.float32)
        + expand_bias[:, None]
    )
    token_act = gelu_tanh(token_pre).astype(jnp.bfloat16)
    token_part = jnp.einsum(
        "bhd,hs->bsd", token_act, token_reduce, preferred_element_type=jnp.float32
    )
    middle = (
        inputs
        + lax.psum(token_part.astype(jnp.bfloat16), "mp").astype(jnp.float32)
        + reduce_bias[:, None]
    )
    second_norm, second_normal, second_inverse = norm_forward(middle, second_gain, second_bias)
    second_rows = second_norm.astype(jnp.bfloat16).reshape(batch * patches, width)
    channel_pre = (
        jnp.dot(second_rows, channel_expand, preferred_element_type=jnp.float32) + channel_bias
    )
    channel_act = gelu_tanh(channel_pre).astype(jnp.bfloat16)
    channel_part = jnp.dot(channel_act, channel_reduce, preferred_element_type=jnp.float32)
    mixed = lax.psum(channel_part.astype(jnp.bfloat16), "mp").astype(jnp.float32) + output_bias
    block_output = (middle + mixed.reshape(batch, patches, width)).astype(jnp.bfloat16)
    upstream = cotangent.astype(jnp.float32)
    cot_rows = cotangent.reshape(batch * patches, width)
    output_bias_gradient = jnp.sum(upstream, axis=(0, 1))
    hidden_grad = jnp.dot(cot_rows, channel_reduce.T, preferred_element_type=jnp.float32)
    channel_pre_grad = gelu_back(channel_pre, hidden_grad).astype(jnp.bfloat16)
    channel_expand_gradient = jnp.dot(
        second_rows.T, channel_pre_grad, preferred_element_type=jnp.float32
    )
    channel_bias_gradient = jnp.sum(channel_pre_grad.astype(jnp.float32), axis=0)
    second_part = jnp.dot(channel_pre_grad, channel_expand.T, preferred_element_type=jnp.float32)
    second_grad = (
        lax.psum(second_part.astype(jnp.bfloat16), "mp")
        .astype(jnp.float32)
        .reshape(batch, patches, width)
    )
    second_gain_gradient = jnp.sum(second_grad * second_normal, axis=(0, 1))
    second_bias_gradient = jnp.sum(second_grad, axis=(0, 1))
    middle_grad = upstream + norm_backward(second_grad, second_normal, second_inverse, second_gain)
    middle_low = middle_grad.astype(jnp.bfloat16)
    reduce_bias_gradient = jnp.sum(middle_low.astype(jnp.float32), axis=(0, 2))
    token_reduce_gradient = jnp.einsum(
        "bhd,bsd->hs", token_act, middle_low, preferred_element_type=jnp.float32
    )
    act_grad = jnp.einsum(
        "bsd,hs->bhd", middle_low, token_reduce, preferred_element_type=jnp.float32
    )
    token_pre_grad = gelu_back(token_pre, act_grad).astype(jnp.bfloat16)
    expand_bias_gradient = jnp.sum(token_pre_grad.astype(jnp.float32), axis=(0, 2))
    token_expand_gradient = jnp.einsum(
        "bsd,bhd->sh", first_low, token_pre_grad, preferred_element_type=jnp.float32
    )
    first_part = jnp.einsum(
        "bhd,sh->bsd", token_pre_grad, token_expand, preferred_element_type=jnp.float32
    )
    first_grad = lax.psum(first_part.astype(jnp.bfloat16), "mp").astype(jnp.float32)
    first_gain_gradient = jnp.sum(first_grad * first_normal, axis=(0, 1))
    first_bias_gradient = jnp.sum(first_grad, axis=(0, 1))
    input_grad = middle_grad + norm_backward(first_grad, first_normal, first_inverse, first_gain)
    summed = (
        lax.psum(first_gain_gradient.astype(jnp.bfloat16), "dp").astype(jnp.float32),
        lax.psum(first_bias_gradient.astype(jnp.bfloat16), "dp").astype(jnp.float32),
        lax.psum(token_expand_gradient.astype(jnp.bfloat16), "dp").astype(jnp.float32),
        lax.psum(expand_bias_gradient.astype(jnp.bfloat16), "dp").astype(jnp.float32),
        lax.psum(token_reduce_gradient.astype(jnp.bfloat16), "dp").astype(jnp.float32),
        lax.psum(reduce_bias_gradient.astype(jnp.bfloat16), "dp").astype(jnp.float32),
        lax.psum(second_gain_gradient.astype(jnp.bfloat16), "dp").astype(jnp.float32),
        lax.psum(second_bias_gradient.astype(jnp.bfloat16), "dp").astype(jnp.float32),
        lax.psum(channel_expand_gradient.astype(jnp.bfloat16), "dp").astype(jnp.float32),
        lax.psum(channel_bias_gradient.astype(jnp.bfloat16), "dp").astype(jnp.float32),
        lax.psum(output_bias_gradient.astype(jnp.bfloat16), "dp").astype(jnp.float32),
    )
    per_image = jnp.einsum(
        "bsf,bsd->bfd",
        channel_act.reshape(batch, patches, -1),
        cotangent,
        preferred_element_type=jnp.float32,
    )
    group_range = jnp.arange(GROUPS, dtype=jnp.int32)[None, :]
    dp_count = lax.axis_size("dp")
    member = (group_ids == group_range).astype(jnp.float32)
    per_group = jnp.einsum("bk,bfd->kfd", member, per_image, precision=highest)
    received = lax.all_to_all(
        per_group.astype(jnp.bfloat16), "dp", split_axis=2, concat_axis=1, tiled=True
    ).astype(per_group.dtype)
    count_items = received.shape[0]
    pieces = received.reshape(
        count_items, dp_count, received.shape[1] // dp_count, received.shape[2]
    ).sum(axis=1)
    squares = jnp.sum(pieces * pieces, axis=(1, 2))
    products = jnp.sum(pieces * query_gradient, axis=(1, 2))
    channel_reduce_gradient = jnp.sum(pieces, axis=0)
    totals = lax.psum((squares, products), ("dp", "mp"))
    norm_raw = jnp.sqrt(totals[0])
    average = jnp.mean(norm_raw)
    factor = average / jnp.maximum(norm_raw, average)
    influence = factor * totals[1] / average
    group_norms = norm_raw / average
    return (
        block_output,
        input_grad,
        summed[0],
        summed[1],
        summed[2],
        summed[3],
        summed[4],
        summed[5],
        summed[6],
        summed[7],
        summed[8],
        summed[9],
        channel_reduce_gradient,
        summed[10],
        group_norms,
        influence,
    )


def solution(mesh):
    in_specs = (
        P("dp", None, None),
        P("dp", None),
        P("mp", "dp"),
        P(),
        P(),
        P(None, "mp"),
        P("mp"),
        P("mp", None),
        P(),
        P(),
        P(),
        P(None, "mp"),
        P("mp"),
        P("mp", None),
        P(),
        P("dp", None, None),
    )
    out_specs = (
        P("dp", None, None),
        P("dp", None, None),
        P(),
        P(),
        P(None, "mp"),
        P("mp"),
        P("mp", None),
        P(),
        P(),
        P(),
        P(None, "mp"),
        P("mp"),
        P("mp", "dp"),
        P(),
        P(),
        P(),
    )
    return jax.shard_map(
        per_device, mesh=mesh, in_specs=in_specs, out_specs=out_specs, check_vma=False
    )
```

profile of v0, /device:TPU:0, one launch (start us, length us, event | category | flops | bytes accessed | tf_op | source)
XLA Modules:
  0.0 939.5 jit_solution(2422784996029551318)
XLA Ops:
  7.3 2.5 convert_reduce_fusion
  9.8 2.6 fusion.18
  12.6 1.4 fusion.42
  14.1 2.8 convert_bitcast_fusion.1
  16.9 60.1 %all-reduce.9.cloned.1.call-done = bf16[8,196,768]{2,1,0:T(8,128)(2,1)} async-done(((bf16[8,196,768]{2,1,0:T(8,128)(2,1)}), bf16[8,196,768]{2,1,0:T(8,128)(2,1)}) %all-reduce.9.cloned.1.call-update) | async-done | bytes 2408464 | tf_op jit(solution)/shard_map/psum | solution.py:70
  77.0 3.5 fusion.67
  80.9 1.8 multiply_reduce_fusion.2
  82.7 0.6 copy-done.12
  83.3 2.7 add_convert_fusion.1
  86.0 4.1 reshape.105
  90.0 7.6 multiply_convert_fusion
  97.7 4.1 reshape.109
  101.8 5.2 fusion.63
  106.9 23.8 %fusion.2 = bf16[16,768,768]{2,0,1:T(8,128)(2,1)} fusion(f32[8,768,768]{2,1,0:T(8,128)S(1)} %fusion.63, s32[8]{0:T(128)S(1)} %bitcast.77), kind=kOutput, calls=%fused_computation.3 | convolution fusion | flops 915406976 | bytes 37748768 | tf_op jit(solution)/shard_map/bk,bfd->kfd/dot_general | solution.py:142
  130.8 27.0 %copy.60 = bf16[16,768,768]{1,0,2:T(8,128)(2,1)} copy(bf16[16,768,768]{2,0,1:T(8,128)(2,1)} %fusion.2) | data formatting | bytes 37748736 | tf_op jit(solution)/shard_map/convert_element_type | solution.py:144
  157.8 5.9 all-to-all-start
  163.7 3.7 copy.56
  167.4 4.1 reshape.107
  171.5 8.8 fusion.68
  180.3 1.5 copy-done.35
  181.8 3.5 convolution_convert_fusion
  185.4 5.8 convolution_convert_fusion.2
  191.7 5.5 convolution_convert_fusion.1
  197.2 45.3 %all-reduce.11.cloned.1.call-done = bf16[1568,768]{1,0:T(8,128)(2,1)} async-done(((bf16[1568,768]{1,0:T(8,128)(2,1)}), bf16[1568,768]{1,0:T(8,128)(2,1)}) %all-reduce.11.cloned.1.call-update) | async-done | bytes 2408464 | tf_op jit(solution)/shard_map/psum | solution.py:93
  242.5 2.2 multiply_reduce_fusion.3
  244.8 4.5 reshape.108
  249.4 7.6 multiply_reduce_fusion
  257.0 5.9 convert_reduce_fusion.1
  262.9 2.7 fusion.70
  265.6 2.3 convert_bitcast_fusion
  268.0 2.7 reduce_sum.232
  270.7 359.9 %all-reduce.13.cloned.1.call-done = bf16[768,768]{1,0:T(8,128)(2,1)} async-done(((bf16[768,768]{1,0:T(8,128)(2,1)}), bf16[768,768]{1,0:T(8,128)(2,1)}) %all-reduce.13.cloned.1.call-update) | async-done | bytes 1179664 | tf_op jit(solution)/shard_map/psum | solution.py:129
  630.6 2.8 convert_element_type.162
  633.4 2.7 reduce_sum.227
  636.2 4.0 fusion.48
  640.3 0.5 copy-done.10
  640.8 1.8 fusion.47
  642.6 87.0 %all-reduce.17.cloned.1.call-done = (bf16[1568,768]{1,0:T(8,128)(2,1)}, bf16[8,196,768]{2,1,0:T(8,128)(2,1)}) async-done(((bf16[1568,768]{1,0:T(8,128)(2,1)}, bf16[8,196,768]{2,1,0:T(8,128)(2,1)}), (bf16[1568,768]{1,0:T(8,128)(2,1)}, bf16[8,196,768]{2,1,0:T(8,128)(2,1)})) %all-reduce.17.cloned.1.call-update) | async-done | bytes 4816912 | tf_op jit(solution)/shard_map/psum | solution.py:80
  729.6 2.7 reduce_sum.223
  732.3 4.2 convert_add_fusion.1
  736.6 5.4 reshape.106
  742.0 6.4 fusion.20
  748.4 7.3 fusion.17
  755.7 3.7 copy.65
  759.4 1.9 copy.64
  761.3 59.1 %all-reduce.15.cloned.1.call-done = (bf16[768]{0:T(1024)(128)(2,1)}, bf16[768]{0:T(1024)(128)(2,1)}, bf16[196,96]{0,1:T(8,128)(2,1)}, bf16[96]{0:T(256)(128)(2,1...) async-done(((bf16[768]{0:T(1024)(128)(2,1)}, ...) | async-done | bytes 85080 | tf_op jit(solution)/shard_map/psum | solution.py:121
  820.4 1.1 convert_element_type.154
  821.5 1.2 convert_element_type.157
  822.8 1.2 convert_element_type.150
  824.0 1.3 convert_element_type.151
  825.2 1.2 convert_element_type.159
  826.5 1.3 convert_element_type.160
  827.7 1.2 convert_element_type.163
  829.0 1.2 convert_element_type.166
  830.2 1.4 convert_element_type.153
  831.7 1.4 convert_element_type.156
  833.1 14.1 %fusion.5 = f32[768,768]{0,1:T(8,128)S(1)} fusion(bf16[16,768,768]{1,0,2:T(8,128)(2,1)} %all-to-all-done), kind=kLoop, calls=%fused_computation.7 | loop fusion | flops 18284544 | bytes 21233664 | tf_op jit(solution)/shard_map/reduce_sum | solution.py:152
  847.2 0.8 reduce_sum.231
  848.1 22.4 %copy_convert_fusion = f32[16,768,768]{1,2,0:T(8,128)} fusion(bf16[16,768,768]{1,0,2:T(8,128)(2,1)} %all-to-all-done), kind=kLoop, calls=%fused_computation | loop fusion | flops 9437184 | bytes 56623104 | tf_op jit(solution)/shard_map/convert_element_type | solution.py:145
  870.5 17.0 %reduce_sum.233 = f32[16,768,96]{1,2,0:T(8,128)} reduce(f32[16,768,8,96]{1,3,2,0:T(8,128)} %bitcast.73, f32[]{:T(128)} %constant.31.clone.1), dimensions={2}, to_apply=%region_33.0 | reduce | flops 8257536 | bytes 42467332 | tf_op jit(solution)/shard_map/reduce_sum | solution.py:149
  887.5 3.1 multiply_reduce_fusion.4
  890.6 40.4 %all-reduce = (f32[16]{0:T(128)S(1)}, f32[16]{0:T(128)S(1)}) all-reduce(f32[16]{0:T(128)S(1)} %get-tuple-element.85, f32[16]{0:T(128)S(1)} %get-tuple-element.84), channel_id=1, replica_groups=mesh['dp'=8,'mp'=4] {'dp','mp'}, use_global_device_ids=true, to_apply=%region_35.0 | all-reduce | flops 32 | bytes 256 | tf_op jit(solution)/shard_map/psum | solution.py:153
  931.0 0.6 sqrt_reduce_fusion
  932.3 0.5 fusion.60
  (93 shorter events, 1.4 us)
Async XLA Ops:
  7.2 82.9 %copy-start = (bf16[768,768]{1,0:T(8,128)(2,1)S(1)}, bf16[768,768]{1,0:T(8,128)(2,1)}, u32[]{:S(2)}) copy-start(bf16[768,768]{1,0:T(8,128)(2,1)} %param.27) | copy-start | bytes 3538948
  7.2 69.8 %all-reduce.9.cloned.1.call-start = ((), (), s32[]{:S(2)}) async-start(), calls=%async_computation.1 | async-start | bytes 4915200 | tf_op jit(solution)/shard_map/psum | solution.py:70
  7.2 5.3 copy-start.2
  7.3 5.3 copy-start.18
  7.3 5.3 copy-start.23
  7.3 5.3 copy-start.33
  12.5 1.5 copy-start.27
  12.5 1.5 copy-start.31
  12.6 4.3 copy-start.14
  14.1 248.9 %copy-start.9 = (f32[8,768,96]{1,2,0:T(8,128)}, f32[8,768,96]{1,2,0:T(8,128)S(1)}, u32[]{:S(2)}) copy-start(f32[8,768,96]{1,2,0:T(8,128)S(1)} %fusion.42) | copy-start | bytes 7077892
  77.0 3.5 copy-start.3
  77.0 3.9 copy-start.5
  77.0 3.9 copy-start.20
  77.0 6.3 copy-start.16
  77.0 6.3 copy-start.25
  82.7 0.6 copy-start.12
  101.7 5.2 copy-start.30
  157.8 675.3 %all-to-all-start = ((bf16[16,768,768]{1,0,2:T(8,128)(2,1)}), bf16[16,768,768]{1,0,2:T(8,128)(2,1)}, u32[]{:S(2)}, u32[]{:S(2)}) async-start(bf16[16,768,768]{1,0,2:T(8,128)(2,1)} %copy.60), calls=%async_computation | async-start | bytes 37748736 | tf_op jit(solution)/shard_map/all_to_all | solution.py:143
  163.7 78.8 %all-reduce.11.cloned.1.call-start = ((), (), s32[]{:S(2)}) async-start(), calls=%async_computation.2 | async-start | bytes 4816896 | tf_op jit(solution)/shard_map/psum | solution.py:93
  180.3 1.5 copy-start.35
  185.4 445.2 %all-reduce.13.cloned.1.call-start = ((), (), s32[]{:S(2)}) async-start(), calls=%async_computation.3 | async-start | bytes 2359296 | tf_op jit(solution)/shard_map/psum | solution.py:129
  191.2 51.3 %copy-start.17 = (f32[768]{0:T(1024)S(1)}, f32[768]{0:T(1024)}, u32[]{:S(2)}) copy-start(f32[768]{0:T(1024)} %param.25) | copy-start | bytes 9220
  191.2 538.4 %all-reduce.17.cloned.1.call-start = ((), (), s32[]{:S(2)}) async-start(), calls=%async_computation.5 | async-start | bytes 9732096 | tf_op jit(solution)/shard_map/psum | solution.py:80
  197.2 52.2 %copy-start.13 = (f32[8,196]{1,0:T(8,128)S(1)}, f32[8,196]{1,0:T(8,128)}, u32[]{:S(2)}) copy-start(f32[8,196]{1,0:T(8,128)} %copy-done.12) | copy-start | bytes 18820
  197.2 52.2 %copy-start.21 = (f32[196]{0:T(256)S(1)}, f32[196]{0:T(256)}, u32[]{:S(2)}) copy-start(f32[196]{0:T(256)} %param.24) | copy-start | bytes 2356
  249.4 7.6 copy-start.4
  249.4 7.6 copy-start.6
  249.4 7.6 copy-start.7
  257.0 5.9 copy-start.28
  257.0 5.9 copy-start.32
  262.9 2.7 copy-start.8
  262.9 2.7 copy-start.19
  267.9 368.2 %copy-start.15 = (f32[8,196]{1,0:T(8,128)S(1)}, f32[8,196]{1,0:T(8,128)}, u32[]{:S(2)}) copy-start(f32[8,196]{1,0:T(8,128)} %copy-done.14) | copy-start | bytes 18820
  268.0 368.2 %copy-start.24 = (f32[768]{0:T(1024)S(1)}, f32[768]{0:T(1024)}, u32[]{:S(2)}) copy-start(f32[768]{0:T(1024)} %param.19) | copy-start | bytes 9220
  268.0 368.2 %copy-start.34 = (f32[768]{0:T(1024)S(1)}, f32[768]{0:T(1024)}, u32[]{:S(2)}) copy-start(f32[768]{0:T(1024)} %param.20) | copy-start | bytes 9220
  268.0 552.4 %all-reduce.15.cloned.1.call-start = ((), (), s32[]{:S(2)}) async-start(), calls=%async_computation.4 | async-start | bytes 223232 | tf_op jit(solution)/shard_map/psum | solution.py:121
  633.4 6.8 slice-start
  636.2 4.1 slice-start.1
  636.2 4.6 copy-start.10
  636.2 4.6 copy-start.29
  640.8 91.6 %copy-start.26 = (f32[768]{0:T(1024)S(1)}, f32[768]{0:T(1024)}, u32[]{:S(2)}) copy-start(f32[768]{0:T(1024)} %param.30) | copy-start | bytes 9220
  741.9 6.4 copy-start.22
  870.5 17.0 %copy-start.11 = (f32[768,96]{0,1:T(8,128)S(1)}, f32[768,96]{0,1:T(8,128)}, u32[]{:S(2)}) copy-start(f32[768,96]{0,1:T(8,128)} %param.18) | copy-start | bytes 884740
  870.5 62.3 %copy-start.1 = (bf16[768,768]{1,0:T(8,128)(2,1)S(1)}, bf16[768,768]{1,0:T(8,128)(2,1)}, u32[]{:S(2)}) copy-start(bf16[768,768]{1,0:T(8,128)(2,1)} %param.27) | copy-start | bytes 3538948
Sparse Core Ops, SparseCore 0:
  17.0 59.9 all-reduce.8
  185.5 56.9 all-reduce.10
  247.0 383.5 all-reduce.12
  633.5 96.1 all-reduce.16
  748.5 71.8 all-reduce.14
where the time goes:
time: 946 us; the launch traced here: 940 us
  waiting for transfers between devices  612 us (65%)
  other arithmetic  129 us (14%)
  matrix products  75.2 us (8%)
  local copies, waits for them, and re-layouts  61.7 us (7%)
  blocking collectives  40.4 us (4%)
  between operations  15 us (2%)
    psum x1, waiting for transfers between devices, per_device(): lax.psum(channel_expand_gradient.astype(jnp.bfloat16), 'dp')  360 us
    psum x1, waiting for transfers between devices, per_device(): lax.psum(channel_part.astype(jnp.bfloat16), 'mp').astype(jnp.float32)  87 us
    psum x1, waiting for transfers between devices, per_device(): lax.psum(token_part.astype(jnp.bfloat16), 'mp').astype(jnp.float32)  60.1 us
    psum x1, waiting for transfers between devices, per_device(): lax.psum(first_gain_gradient.astype(jnp.bfloat16), 'dp').astype(jnp.float32)  59.1 us
    psum x1, waiting for transfers between devices, per_device(): lax.psum(second_part.astype(jnp.bfloat16), 'mp').astype(jnp.float32)  45.3 us
    psum x1, blocking collectives, per_device(): totals = lax.psum((squares, products), ('dp', 'mp'))  40.4 us
    convert_element_type x1, local copies, waits for them, and re-layouts, per_device(): per_group.astype(jnp.bfloat16)  27 us
    dot_general x1, matrix products, per_device(): per_group = jnp.einsum('bk,bfd->kfd', member, per_image, precision=highest)  23.8 us
  transfers between devices with their start and end apart: 6, of which 5 were waited for; matrix products, arithmetic and copies ran while one was open for 12% of the time, Pallas kernels for 0%

commit v1 on v0

--- a/solution.py
+++ b/solution.py
@@ -126,7 +126,9 @@
         lax.psum(reduce_bias_gradient.astype(jnp.bfloat16), "dp").astype(jnp.float32),
         lax.psum(second_gain_gradient.astype(jnp.bfloat16), "dp").astype(jnp.float32),
         lax.psum(second_bias_gradient.astype(jnp.bfloat16), "dp").astype(jnp.float32),
-        lax.psum(channel_expand_gradient.astype(jnp.bfloat16), "dp").astype(jnp.float32),
+        jnp.sum(lax.all_gather(channel_expand_gradient.astype(jnp.bfloat16), "dp"), axis=0).astype(
+            jnp.float32
+        ),
         lax.psum(channel_bias_gradient.astype(jnp.bfloat16), "dp").astype(jnp.float32),
         lax.psum(output_bias_gradient.astype(jnp.bfloat16), "dp").astype(jnp.float32),
     )

time: 946 us -> 887 us (0.938)
  waiting for transfers between devices: 612 us -> 550 us
    psum x1 -> x0, waiting for transfers between devices: 360 us -> none  [per_device(): lax.psum(channel_expand_gradient.astype(jnp.bfloat16), 'dp')]
    psum x1, waiting for transfers between devices: 59.1 us -> 225 us  [per_device(): lax.psum(first_gain_gradient.astype(jnp.bfloat16), 'dp').astype(jnp.float32)]
    all_gather x0 -> x1, waiting for transfers between devices: none -> 128 us  [per_device(): lax.all_gather(channel_expand_gradient.astype(jnp.bfloat16), 'dp')]
  transfers between devices with their start and end apart: 6 -> 6, of which waited for: 5 -> 5; matrix products, arithmetic and copies ran while one was open for 12% -> 14% of each run, Pallas kernels for 0% -> 0%
where the time goes in v1:
time: 887 us; the launch traced here: 881 us
  waiting for transfers between devices  550 us (62%)
  other arithmetic  134 us (15%)
  matrix products  75.4 us (9%)
  local copies, waits for them, and re-layouts  61.4 us (7%)
  blocking collectives  38.4 us (4%)
  between operations  15 us (2%)
    psum x1, waiting for transfers between devices, per_device(): lax.psum(first_gain_gradient.astype(jnp.bfloat16), 'dp').astype(jnp.float32)  225 us
    all_gather x1, waiting for transfers between devices, per_device(): lax.all_gather(channel_expand_gradient.astype(jnp.bfloat16), 'dp')  128 us
    psum x1, waiting for transfers between devices, per_device(): lax.psum(channel_part.astype(jnp.bfloat16), 'mp').astype(jnp.float32)  85.3 us
    psum x1, waiting for transfers between devices, per_device(): lax.psum(token_part.astype(jnp.bfloat16), 'mp').astype(jnp.float32)  60.1 us
    psum x1, waiting for transfers between devices, per_device(): lax.psum(second_part.astype(jnp.bfloat16), 'mp').astype(jnp.float32)  51.6 us
    psum x1, blocking collectives, per_device(): totals = lax.psum((squares, products), ('dp', 'mp'))  38.4 us
    convert_element_type x1, local copies, waits for them, and re-layouts, per_device(): per_group.astype(jnp.bfloat16)  27 us
    dot_general x1, matrix products, per_device(): per_group = jnp.einsum('bk,bfd->kfd', member, per_image, precision=highest)  23.8 us
  transfers between devices with their start and end apart: 6, of which 5 were waited for; matrix products, arithmetic and copies ran while one was open for 14% of the time, Pallas kernels for 0%

profile of v1, /device:TPU:0, one launch (start us, length us, event | category | flops | bytes accessed | tf_op | source)
XLA Modules:
  0.0 880.6 jit_solution(5580964205388207548)
XLA Ops:
  7.3 2.5 convert_reduce_fusion
  9.9 2.7 fusion.18
  12.6 1.4 fusion.42
  14.1 2.8 convert_bitcast_fusion.1
  16.9 60.1 %all-reduce.8.cloned.1.call-done = bf16[8,196,768]{2,1,0:T(8,128)(2,1)} async-done(((bf16[8,196,768]{2,1,0:T(8,128)(2,1)}), bf16[8,196,768]{2,1,0:T(8,128)(2,1)}) %all-reduce.8.cloned.1.call-update) | async-done | bytes 2408464 | tf_op jit(solution)/shard_map/psum | solution.py:70
  77.0 3.5 fusion.67
  80.9 1.8 multiply_reduce_fusion.2
  82.7 0.6 copy-done.12
  83.3 2.7 add_convert_fusion.1
  86.0 4.1 reshape.105
  90.1 7.6 multiply_convert_fusion
  97.7 4.1 reshape.109
  101.8 5.2 fusion.63
  106.9 23.8 %fusion.2 = bf16[16,768,768]{2,0,1:T(8,128)(2,1)} fusion(f32[8,768,768]{2,1,0:T(8,128)S(1)} %fusion.63, s32[8]{0:T(128)S(1)} %bitcast.79), kind=kOutput, calls=%fused_computation.3 | convolution fusion | flops 915406976 | bytes 37748768 | tf_op jit(solution)/shard_map/bk,bfd->kfd/dot_general | solution.py:144
  130.8 27.0 %copy.60 = bf16[16,768,768]{1,0,2:T(8,128)(2,1)} copy(bf16[16,768,768]{2,0,1:T(8,128)(2,1)} %fusion.2) | data formatting | bytes 37748736 | tf_op jit(solution)/shard_map/convert_element_type | solution.py:146
  157.8 5.9 all-to-all-start
  163.7 3.7 copy.56
  167.4 4.1 reshape.107
  171.5 8.8 fusion.68
  180.3 1.5 copy-done.35
  181.8 3.5 convolution_convert_fusion
  185.3 5.5 convolution_convert_fusion.1
  190.9 51.6 %all-reduce.10.cloned.1.call-done = bf16[1568,768]{1,0:T(8,128)(2,1)} async-done(((bf16[1568,768]{1,0:T(8,128)(2,1)}), bf16[1568,768]{1,0:T(8,128)(2,1)}) %all-reduce.10.cloned.1.call-update) | async-done | bytes 2408464 | tf_op jit(solution)/shard_map/psum | solution.py:93
  242.4 2.2 multiply_reduce_fusion.3
  244.8 4.9 reshape.108
  249.7 7.8 multiply_reduce_fusion
  257.5 5.9 convert_reduce_fusion.1
  263.4 2.7 fusion.70
  266.1 2.3 convert_bitcast_fusion
  268.5 2.7 reduce_sum.245
  271.1 2.7 reduce_sum.239
  273.9 4.3 fusion.48
  278.2 1.8 fusion.47
  280.0 85.3 %all-reduce.14.cloned.1.call-done = (bf16[1568,768]{1,0:T(8,128)(2,1)}, bf16[8,196,768]{2,1,0:T(8,128)(2,1)}) async-done(((bf16[1568,768]{1,0:T(8,128)(2,1)}, bf16[8,196,768]{2,1,0:T(8,128)(2,1)}), (bf16[1568,768]{1,0:T(8,128)(2,1)}, bf16[8,196,768]{2,1,0:T(8,128)(2,1)})) %all-reduce.14.cloned.1.call-update) | async-done | bytes 4816912 | tf_op jit(solution)/shard_map/psum | solution.py:80
  365.3 2.7 reduce_sum.235
  368.0 6.4 fusion.20
  374.7 5.8 convolution_convert_fusion.2
  380.5 4.2 convert_add_fusion.1
  384.7 5.3 reshape.106
  390.0 7.3 fusion.17
  397.3 3.7 copy.65
  401.0 1.9 copy.64
  402.8 225.1 %all-reduce.12.cloned.1.call-done = (bf16[768]{0:T(1024)(128)(2,1)}, bf16[768]{0:T(1024)(128)(2,1)}, bf16[196,96]{0,1:T(8,128)(2,1)}, bf16[96]{0:T(256)(128)(2,1...) async-done(((bf16[768]{0:T(1024)(128)(2,1)}, ...) | async-done | bytes 85080 | tf_op jit(solution)/shard_map/psum | solution.py:121
  627.9 1.1 convert_element_type.156
  629.0 1.2 convert_element_type.159
  630.2 1.3 convert_element_type.152
  631.5 1.3 convert_element_type.153
  632.8 1.3 convert_element_type.161
  634.0 1.3 convert_element_type.162
  635.3 1.3 convert_element_type.165
  636.6 1.3 convert_element_type.168
  637.9 1.5 convert_element_type.155
  639.3 1.5 convert_element_type.158
  640.8 128.2 %all-gather.3.cloned.1.call-done = bf16[6144,768]{1,0:T(8,128)(2,1)} async-done(((bf16[768,768]{1,0:T(8,128)(2,1)}), bf16[6144,768]{1,0:T(8,128)(2,1)}) %all-gather.3.cloned.1.call-update) | async-done | bytes 9437200 | tf_op jit(solution)/shard_map/all_gather | solution.py:129
  768.9 5.7 reduce_sum.240
  774.6 1.6 convert_element_type.164
  776.2 14.1 %fusion.5 = f32[768,768]{0,1:T(8,128)S(1)} fusion(bf16[16,768,768]{1,0,2:T(8,128)(2,1)} %all-to-all-done), kind=kLoop, calls=%fused_computation.7 | loop fusion | flops 18284544 | bytes 21233664 | tf_op jit(solution)/shard_map/reduce_sum | solution.py:154
  790.4 0.8 reduce_sum.244
  791.2 22.4 %copy_convert_fusion = f32[16,768,768]{1,2,0:T(8,128)} fusion(bf16[16,768,768]{1,0,2:T(8,128)(2,1)} %all-to-all-done), kind=kLoop, calls=%fused_computation | loop fusion | flops 9437184 | bytes 56623104 | tf_op jit(solution)/shard_map/convert_element_type | solution.py:147
  813.6 17.0 %reduce_sum.246 = f32[16,768,96]{1,2,0:T(8,128)} reduce(f32[16,768,8,96]{1,3,2,0:T(8,128)} %bitcast.74, f32[]{:T(128)} %constant.32.clone.1), dimensions={2}, to_apply=%region_33.0 | reduce | flops 8257536 | bytes 42467332 | tf_op jit(solution)/shard_map/reduce_sum | solution.py:151
  830.6 3.1 multiply_reduce_fusion.4
  833.7 38.4 %all-reduce = (f32[16]{0:T(128)S(1)}, f32[16]{0:T(128)S(1)}) all-reduce(f32[16]{0:T(128)S(1)} %get-tuple-element.85, f32[16]{0:T(128)S(1)} %get-tuple-element.84), channel_id=1, replica_groups=mesh['dp'=8,'mp'=4] {'dp','mp'}, use_global_device_ids=true, to_apply=%region_35.0 | all-reduce | flops 32 | bytes 256 | tf_op jit(solution)/shard_map/psum | solution.py:155
  872.1 0.6 sqrt_reduce_fusion
  873.4 0.5 fusion.60
  (94 shorter events, 1.2 us)
Async XLA Ops:
  7.2 82.9 %copy-start = (bf16[768,768]{1,0:T(8,128)(2,1)S(1)}, bf16[768,768]{1,0:T(8,128)(2,1)}, u32[]{:S(2)}) copy-start(bf16[768,768]{1,0:T(8,128)(2,1)} %param.27) | copy-start | bytes 3538948
  7.2 69.8 %all-reduce.8.cloned.1.call-start = ((), (), s32[]{:S(2)}) async-start(), calls=%async_computation.1 | async-start | bytes 4915200 | tf_op jit(solution)/shard_map/psum | solution.py:70
  7.2 5.3 copy-start.2
  7.3 5.3 copy-start.18
  7.3 5.3 copy-start.23
  7.3 5.3 copy-start.33
  9.8 4.2 copy-start.27
  9.9 4.2 copy-start.31
  12.6 4.3 copy-start.14
  14.1 249.3 %copy-start.9 = (f32[8,768,96]{1,2,0:T(8,128)}, f32[8,768,96]{1,2,0:T(8,128)S(1)}, u32[]{:S(2)}) copy-start(f32[8,768,96]{1,2,0:T(8,128)S(1)} %fusion.42) | copy-start | bytes 7077892
  77.0 3.5 copy-start.3
  77.0 3.9 copy-start.5
  77.0 3.9 copy-start.20
  77.0 6.3 copy-start.16
  77.0 6.3 copy-start.25
  82.7 0.6 copy-start.12
  101.8 5.2 copy-start.30
  157.8 618.5 %all-to-all-start = ((bf16[16,768,768]{1,0,2:T(8,128)(2,1)}), bf16[16,768,768]{1,0,2:T(8,128)(2,1)}, u32[]{:S(2)}, u32[]{:S(2)}) async-start(bf16[16,768,768]{1,0,2:T(8,128)(2,1)} %copy.60), calls=%async_computation | async-start | bytes 37748736 | tf_op jit(solution)/shard_map/all_to_all | solution.py:145
  163.7 78.7 %all-reduce.10.cloned.1.call-start = ((), (), s32[]{:S(2)}) async-start(), calls=%async_computation.2 | async-start | bytes 4816896 | tf_op jit(solution)/shard_map/psum | solution.py:93
  180.3 1.5 copy-start.35
  185.3 57.1 %copy-start.17 = (f32[768]{0:T(1024)S(1)}, f32[768]{0:T(1024)}, u32[]{:S(2)}) copy-start(f32[768]{0:T(1024)} %param.25) | copy-start | bytes 9220
  185.3 180.0 %all-reduce.14.cloned.1.call-start = ((), (), s32[]{:S(2)}) async-start(), calls=%async_computation.5 | async-start | bytes 9732096 | tf_op jit(solution)/shard_map/psum | solution.py:80
  190.9 58.8 %copy-start.13 = (f32[8,196]{1,0:T(8,128)S(1)}, f32[8,196]{1,0:T(8,128)}, u32[]{:S(2)}) copy-start(f32[8,196]{1,0:T(8,128)} %copy-done.12) | copy-start | bytes 18820
  190.9 58.8 %copy-start.21 = (f32[196]{0:T(256)S(1)}, f32[196]{0:T(256)}, u32[]{:S(2)}) copy-start(f32[196]{0:T(256)} %param.24) | copy-start | bytes 2356
  249.7 7.8 copy-start.4
  249.7 7.8 copy-start.6
  249.7 7.8 copy-start.7
  257.5 5.9 copy-start.28
  257.5 5.9 copy-start.32
  263.4 2.7 copy-start.8
  263.4 2.7 copy-start.19
  268.4 5.5 copy-start.15
  268.4 5.5 copy-start.24
  268.4 5.5 copy-start.34
  268.4 359.5 %all-reduce.12.cloned.1.call-start = ((), (), s32[]{:S(2)}) async-start(), calls=%async_computation.4 | async-start | bytes 223232 | tf_op jit(solution)/shard_map/psum | solution.py:121
  271.1 7.1 slice-start
  273.9 4.3 slice-start.1
  273.9 4.3 copy-start.10
  273.9 4.3 copy-start.29
  374.4 6.1 copy-start.26
  374.4 394.5 %all-gather.3.cloned.1.call-start = ((), (), s32[]{:S(2)}) async-start(), calls=%async_computation.3 | async-start | bytes 10616832 | tf_op jit(solution)/shard_map/all_gather | solution.py:129
  384.7 5.3 copy-start.22
  813.6 17.0 %copy-start.11 = (f32[768,96]{0,1:T(8,128)S(1)}, f32[768,96]{0,1:T(8,128)}, u32[]{:S(2)}) copy-start(f32[768,96]{0,1:T(8,128)} %param.18) | copy-start | bytes 884740
  813.6 60.3 %copy-start.1 = (bf16[768,768]{1,0:T(8,128)(2,1)S(1)}, bf16[768,768]{1,0:T(8,128)(2,1)}, u32[]{:S(2)}) copy-start(bf16[768,768]{1,0:T(8,128)(2,1)} %param.27) | copy-start | bytes 3538948
Sparse Core Ops, SparseCore 0:
  17.0 59.9 all-reduce.7
  185.4 56.9 all-reduce.9
  268.5 96.7 all-reduce.13
  374.6 253.3 all-reduce.11
  630.8 138.1 all-gather.2
